TPU v7x, 256 devices: a whole 4x4x8 slice. The times are simulated.
256 devices in a mesh: blk: 128 (over y, z, x), rep: 2 (over core).
Axes of the slice: x: 4, y: 4, z: 8, core: 2. Of those that a mesh axis runs over, the one named last changes fastest.
Arguments:
- features: bfloat16 [32768, 256], P('blk', 'rep'), may hold values from -6 to 6
- observations: bfloat16 [256, 128], P('blk'), may hold values from -6 to 6
- cond_ids: int32 [256, 4], P('blk'), may hold values from 0 to 255, as said below
Outputs:
- block_loglik: float32 [256], P(('blk', 'rep'))
- feature_grad: float32 [32768, 256], P('blk', 'rep')
Inputs may be any that keep to these rules, and one draw needn't show every extreme that they name: `cond_ids`: row b names 4 different blocks, none of them b. Entry 0 is block (b - 1) mod 256; entry 1 is block (b - a) mod 256 for some a from 2 to 4; the remaining entries of all rows together name exactly 8 distinct blocks.
All inputs are finite; a program needn't handle non-finite values.
Results may differ from a plain program's by a relative error of at most 0.017.
Values may be sent and summed in bfloat16 or wider, within the bound.
A program may use at most 64 MiB of HBM per device.

v0:
```python
import math

import jax
import jax.numpy as jnp
from jax import lax
from jax.sharding import PartitionSpec as P

HOT = 8


def from_root(value, axis, source):
    kept = jnp.where(lax.axis_index(axis) == source, value, 0).astype(value.dtype)
    return lax.psum(kept, axis)


def from_behind(array, axis, by):
    length = lax.axis_size(axis)
    return lax.ppermute(array, axis, [(i, (i + by) % length) for i in range(length)])


def block_terms(joint_x, joint_y, own):
    joint = joint_x.shape[0]
    width = joint_x.shape[1]
    wide_x = joint_x.astype(jnp.float32)
    squares = jnp.sum(wide_x * wide_x, axis=1)
    gram = jnp.dot(joint_x, joint_x.T, preferred_element_type=jnp.float32)
    dist = squares[:, None] + squares[None, :] - 2.0 * gram
    diag_mask = jnp.eye(joint, dtype=bool)
    ident = jnp.eye(joint, dtype=jnp.float32)

    def loglik_of(dist_in):
        kern = jnp.where(diag_mask, 1.0, jnp.exp(-dist_in * (0.5 / width)))
        sigma = kern + 0.1 * ident
        chol = jnp.linalg.cholesky(sigma)
        solved = jax.scipy.linalg.solve_triangular(chol, joint_y, lower=True)
        tail = solved[joint - own :]
        logs = jnp.log(jnp.diagonal(chol)[joint - own :])
        return -0.5 * jnp.sum(tail * tail) - jnp.sum(logs) - 0.5 * own * math.log(2.0 * math.pi)

    value, pull = jax.vjp(loglik_of, dist)
    weight = pull(jnp.ones((), dist.dtype))[0]
    sym = (weight + weight.T).astype(jnp.bfloat16)
    rowsum = jnp.sum(sym.astype(jnp.float32), axis=1)
    grad = 2.0 * (
        rowsum[:, None] * wide_x - jnp.dot(sym, joint_x, preferred_element_type=jnp.float32)
    )
    return (value, grad)


def body(features, observations, cond_ids):
    per_dev = cond_ids.shape[0]
    ncond = cond_ids.shape[1]
    points = observations.shape[1]
    half = features.shape[1]
    nblocks = lax.axis_size("blk")
    device = lax.axis_index("blk")
    core = lax.axis_index("rep")
    total_blocks = per_dev * nblocks
    feat_blocks = features.reshape(per_dev, points, half)
    all_ids = jnp.arange(total_blocks, dtype=jnp.int32)
    far_ids = cond_ids[:, 2:].reshape(-1)
    marks = jnp.any(far_ids[:, None] == all_ids[None, :], axis=0).astype(jnp.int32)
    marks = lax.pmax(marks, "blk")
    order_score = marks * (2 * total_blocks) - all_ids
    unused, hot_list = lax.top_k(order_score, HOT)
    hot_owner = hot_list // per_dev
    hot_local = hot_list % per_dev
    local_ids = jnp.arange(per_dev, dtype=jnp.int32)
    owned_mask = (hot_owner == device)[:, None] & (hot_local[:, None] == local_ids[None, :])
    owned = owned_mask.astype(jnp.float32)
    feat_list = []
    obs_list = []
    for slot in range(HOT):
        piece = (feat_blocks[hot_local[slot]], observations[hot_local[slot]])
        got_feat, got_obs = (
            from_root(piece[0], "blk", hot_owner[slot]),
            from_root(piece[1], "blk", hot_owner[slot]),
        )
        feat_list.append(got_feat)
        obs_list.append(got_obs)
    hot_feat = jnp.stack(feat_list)
    hot_obs = jnp.stack(obs_list)
    near_feat = [feat_blocks]
    near_obs = [observations]
    for step_by in (1, 2):
        moved_feat, moved_obs = from_behind((feat_blocks, observations), "blk", step_by)
        near_feat.append(moved_feat)
        near_obs.append(moved_obs)
    pool_half = jnp.concatenate(near_feat + [hot_feat], axis=0)
    pool_obs = jnp.concatenate(near_obs + [hot_obs], axis=0)
    pool_full = lax.all_gather(pool_half, "rep", axis=2, tiled=True)
    width = pool_full.shape[2]
    npool = pool_full.shape[0]
    joint = (ncond + 1) * points
    near_ids = cond_ids[:, :2]
    near_slots = (device - near_ids // per_dev) % nblocks * per_dev + near_ids % per_dev
    hot_match = (cond_ids[:, 2:, None] == hot_list[None, None, :]).astype(jnp.int32)
    hot_slots = 3 * per_dev + jnp.sum(
        hot_match * jnp.arange(HOT, dtype=jnp.int32)[None, None, :], axis=2
    )
    slots = jnp.concatenate([near_slots, hot_slots, local_ids[:, None]], axis=1)
    half_count = per_dev // 2
    first_block = core * half_count
    pool_index = jnp.arange(npool, dtype=jnp.int32)

    def one_block(step, carry):
        grads, values = carry
        chosen = lax.dynamic_index_in_dim(slots, first_block + step, 0, keepdims=False)
        joint_x = pool_full[chosen].reshape(joint, width)
        joint_y = pool_obs[chosen].reshape(joint).astype(jnp.float32)
        value, grad = block_terms(joint_x, joint_y, points)
        select = (chosen[:, None] == pool_index[None, :]).astype(jnp.float32)
        grads = grads + jnp.einsum(
            "sn,spf->npf",
            select,
            grad.reshape(ncond + 1, points, width),
            precision=lax.Precision.HIGHEST,
        )
        values = values.at[step].set(value)
        return (grads, values)

    start = (jnp.zeros((npool, points, width), jnp.float32), jnp.zeros((half_count,), jnp.float32))
    pool_grad, values = lax.fori_loop(0, half_count, one_block, start)
    grad_half = lax.psum_scatter(pool_grad, "rep", scatter_dimension=2, tiled=True)
    own_grad = grad_half[:per_dev]
    for step_by in (1, 2):
        part = grad_half[step_by * per_dev : (step_by + 1) * per_dev]
        own_grad = own_grad + from_behind(part.astype(jnp.bfloat16), "blk", -step_by).astype(
            part.dtype
        )
    hot_back = lax.psum(grad_half[3 * per_dev :], "blk")
    own_grad = own_grad + jnp.einsum(
        "hb,hpf->bpf", owned, hot_back, precision=lax.Precision.HIGHEST
    )
    return (values, own_grad.reshape(per_dev * points, half))


def solution(mesh):
    placed = (P("blk", "rep"), P("blk", None), P("blk", None))
    return jax.shard_map(
        body,
        mesh=mesh,
        in_specs=placed,
        out_specs=(P(("blk", "rep")), P("blk", "rep")),
        check_vma=False,
    )
```

profile of v0, /device:TPU:4, one launch (start us, length us, event | category | flops | bytes accessed | tf_op | source)
XLA Modules:
  0.0 896.7 jit_solution(1620216628874519492)
XLA Ops:
  15.6 26.2 %pmax.7 = s32[256]{0:T(256)S(1)} all-reduce(s32[256]{0:T(256)S(1)} %convert_element_type.59), channel_id=1, replica_groups=mesh['blk'=128,'rep'=2] {'blk'}, use_global_device_ids=true, to_apply=%region_1.0 | all-reduce | flops 256 | bytes 2048 | tf_op jit(solution)/shard_map/pmax | solution.py:63
  41.9 3.2 top_k.11
  72.9 217.1 %all-reduce.8.cloned.1.call-done = (bf16[1,128,128]{2,1,0:T(8,128)(2,1)}, bf16[1,128,128]{2,1,0:T(8,128)(2,1)}, bf16[1,128,128]{2,1,0:T(8,128)(2,1)}, bf16[1,128...) async-done(((bf16[1,128,128]{2,1,0:T(8,128)(2,1)}, ...) | async-done | bytes 264208 | tf_op jit(solution)/shard_map/psum | solution.py:13
  310.8 11.7 %cholesky.132 = f32[128,128]{1,0:T(8,128)S(1)} custom-call(f32[128,128]{1,0:T(8,128)S(1)} %cholesky.337), custom_call_target="Cholesky" | custom-call | tf_op jit(solution)/shard_map/while/body/eval_jaxpr/jvp(jit(cholesky))/cholesky | solution.py:34
  323.1 9.8 %custom-call.60 = f32[1,128,128]{1,2,0:T(8,128)S(1)} custom-call(f32[1,128,128]{2,1,0:T(8,128)S(1)} %get-tuple-element.131), custom_call_target="InvertDiagBlocksLowerTriangular" | custom-call | tf_op jit(solution)/shard_map/while/body/eval_jaxpr/jvp(jit(cholesky))/cholesky | solution.py:34
  334.4 13.2 %cholesky.270 = f32[128,128]{1,0:T(8,128)} custom-call(f32[128,128]{1,0:T(8,128)} %cholesky.341), custom_call_target="Cholesky" | custom-call | tf_op jit(solution)/shard_map/while/body/eval_jaxpr/jvp(jit(cholesky))/cholesky | solution.py:34
  349.5 11.4 %custom-call.61 = f32[1,128,128]{1,2,0:T(8,128)} custom-call(f32[1,128,128]{2,1,0:T(8,128)} %get-tuple-element.128), custom_call_target="InvertDiagBlocksLowerTriangular" | custom-call | tf_op jit(solution)/shard_map/while/body/eval_jaxpr/jvp(jit(cholesky))/cholesky | solution.py:34
  363.2 12.5 %cholesky.291 = f32[128,128]{1,0:T(8,128)S(1)} custom-call(f32[128,128]{1,0:T(8,128)} %cholesky.346), custom_call_target="Cholesky" | custom-call | tf_op jit(solution)/shard_map/while/body/eval_jaxpr/jvp(jit(cholesky))/cholesky | solution.py:34
  377.0 10.6 %custom-call.62 = f32[1,128,128]{1,2,0:T(8,128)S(1)} custom-call(f32[1,128,128]{2,1,0:T(8,128)} %get-tuple-element.125), custom_call_target="InvertDiagBlocksLowerTriangular" | custom-call | tf_op jit(solution)/shard_map/while/body/eval_jaxpr/jvp(jit(cholesky))/cholesky | solution.py:34
  388.4 11.9 %cholesky.310 = f32[128,128]{1,0:T(8,128)S(1)} custom-call(f32[128,128]{1,0:T(8,128)S(1)} %cholesky.351), custom_call_target="Cholesky" | custom-call | tf_op jit(solution)/shard_map/while/body/eval_jaxpr/jvp(jit(cholesky))/cholesky | solution.py:34
  400.9 9.8 %custom-call.63 = f32[1,128,128]{1,2,0:T(8,128)S(1)} custom-call(f32[1,128,128]{2,1,0:T(8,128)S(1)} %get-tuple-element.122), custom_call_target="InvertDiagBlocksLowerTriangular" | custom-call | tf_op jit(solution)/shard_map/while/body/eval_jaxpr/jvp(jit(cholesky))/cholesky | solution.py:34
  411.3 11.7 %cholesky.327 = f32[128,128]{1,0:T(8,128)S(1)} custom-call(f32[128,128]{1,0:T(8,128)S(1)} %convolution_subtract_fusion.10), custom_call_target="Cholesky" | custom-call | tf_op jit(solution)/shard_map/while/body/eval_jaxpr/jvp(jit(cholesky))/cholesky | solution.py:34
  434.4 14.4 %while.3 = (s32[]{:T(128)}, f32[640,640]{1,0:T(8,128)}, s32[5,2]{0,1:T(2,128)S(1)}, f32[5,128,128]{2,1,0:T(8,128)S(1)}, s32[]{:T(128)}) while((s32[]{:T(128)}, f32[640,640]{1,0:T(8,128)}, s32[5,2]{0,1:T(2,128)S(1)}, f32[5,128,128]{2,1,0:T(8,128)S(1)}, s32[]{:T(128)}) %tuple.109), condition=%wide.while_cond.1, body=%wide.while_body.1.sunk | while | flops 2 | bytes 131189 | solution.py:35
  448.8 49.1 %custom-call.64 = f32[5,128,128]{1,2,0:T(8,128)S(1)} custom-call(f32[5,128,128]{2,1,0:T(8,128)S(1)} %get-tuple-element.65), custom_call_target="InvertDiagBlocksLowerTriangular" | custom-call | tf_op jit(solution)/shard_map/while/body/eval_jaxpr/jvp(jit(_solve_triangular))/triangular_solve | solution.py:35
  504.1 5.8 gather_fusion.2
  516.4 34.9 %scatter_fusion = f32[640,640]{1,0:T(8,128)S(1)} fusion(f32[640,640]{1,0:T(8,128)S(1)} %negate_select_fusion, s32[640]{0:T(1024)S(1)} %get-tuple-element.183, f32[640]{0:T(1024)S(1)} %pad.10), kind=kCustom, calls=%fused_computation.3 | custom fusion | flops 640 | bytes 12800 | tf_op jit(solution)/shard_map/while/body/eval_jaxpr/transpose(jvp(jit(diagonal)))/cond/branch_0_fun/scatter-add | solution.py:37
  551.3 7.3 divide_select_fusion
  558.6 9.6 %while.4 = (s32[]{:T(128)}, f32[640,640]{1,0:T(8,128)S(1)}, s32[5,2]{0,1:T(2,128)S(1)}, f32[5,128,128]{2,1,0:T(8,128)S(1)}, s32[]{:T(128)}) while((s32[]{:T(128)}, f32[640,640]{1,0:T(8,128)S(1)}, s32[5,2]{0,1:T(2,128)S(1)}, f32[5,128,128]{2,1,0:T(8,128)S(1)}, s32[]{:T(128)}) %tuple.122), condition=%wide.while_cond.2, body=%wide.while_body.2.sunk | while | flops 2 | bytes 131189 | solution.py:34
  568.2 49.3 %custom-call.65 = f32[5,128,128]{1,2,0:T(8,128)S(1)} custom-call(f32[5,128,128]{2,1,0:T(8,128)S(1)} %get-tuple-element.73), custom_call_target="InvertDiagBlocksLowerTriangular" | custom-call | tf_op jit(solution)/shard_map/while/body/eval_jaxpr/transpose(jvp(jit(cholesky)))/triangular_solve | solution.py:34
  636.1 2.9 copy.21
  638.9 3.6 fusion.4
  649.0 13.7 %reduce-scatter.2.cloned.1.call-done = f32[14,128,128]{2,0,1:T(8,128)} async-done(((f32[14,128,256]{2,0,1:T(8,128)}), f32[14,128,128]{2,0,1:T(8,128)}) %reduce-scatter.2.cloned.1.call-update) | async-done | bytes 917520 | tf_op jit(solution)/shard_map/reduce_scatter | solution.py:124
  665.8 7.1 collective-permute-start.4
  674.7 212.0 %all-reduce.6.cloned.1.call-done = f32[8,128,128]{2,0,1:T(8,128)} async-done(((f32[8,128,128]{2,0,1:T(8,128)}), f32[8,128,128]{2,0,1:T(8,128)}) %all-reduce.6.cloned.1.call-update) | async-done | bytes 524304 | tf_op jit(solution)/shard_map/psum | solution.py:131
  (218 shorter events, 121.7 us)
Async XLA Ops:
  7.2 282.8 %all-reduce.8.cloned.1.call-start = ((), (), s32[]{:S(2)}) async-start(), calls=%async_computation.3 | async-start | bytes 532480 | tf_op jit(solution)/shard_map/psum | solution.py:13
  7.2 65.6 %collective-permute-start = (bf16[2,128,128]{2,1,0:T(8,128)(2,1)}, bf16[2,128,128]{2,1,0:T(8,128)(2,1)S(1)}, u32[]{:S(2)}, u32[]{:S(2)}) collective-permute-start(bf16[2,128,128]{2,1,0:T(8,128)(2,1)} %bitcast.322), channel_id=1, source_target_pairs={{0,2},{2,4},{4,6},{6,8},{8,10},{10,12},{12,14},{14,16},{16,18},{18... | collective-permute-start | bytes 196616 | tf_op jit(solution)/shard_map/ppermute | solution.py:18
  8.5 64.4 %collective-permute-start.1 = (bf16[2,128,128]{2,1,0:T(8,128)(2,1)}, bf16[2,128,128]{2,1,0:T(8,128)(2,1)S(1)}, u32[]{:S(2)}, u32[]{:S(2)}) collective-permute-start(bf16[2,128,128]{2,1,0:T(8,128)(2,1)} %bitcast.323), channel_id=1, source_target_pairs={{0,4},{2,6},{4,8},{6,10},{8,12},{10,14},{12,16},{14,18},{16,20},{1... | collective-permute-start | bytes 196616 | tf_op jit(solution)/shard_map/ppermute | solution.py:18
  10.6 415.8 %collective-permute-start.2 = (bf16[2,128]{1,0:T(2,128)(2,1)}, bf16[2,128]{1,0:T(2,128)(2,1)}, u32[]{:S(2)}, u32[]{:S(2)}) collective-permute-start(bf16[2,128]{1,0:T(2,128)(2,1)} %param.6), channel_id=1, source_target_pairs={{0,2},{2,4},{4,6},{6,8},{8,10},{10,12},{12,14},{14,16},{16,18},{18... | collective-permute-start | bytes 1544 | tf_op jit(solution)/shard_map/ppermute | solution.py:18
  12.7 413.7 %collective-permute-start.3 = (bf16[2,128]{1,0:T(2,128)(2,1)}, bf16[2,128]{1,0:T(2,128)(2,1)}, u32[]{:S(2)}, u32[]{:S(2)}) collective-permute-start(bf16[2,128]{1,0:T(2,128)(2,1)} %param.6), channel_id=1, source_target_pairs={{0,4},{2,6},{4,8},{6,10},{8,12},{10,14},{12,16},{14,18},{16,20},{1... | collective-permute-start | bytes 1544 | tf_op jit(solution)/shard_map/ppermute | solution.py:18
  69.9 592.9 %reduce-scatter.2.cloned.1.call-start = ((), (), s32[]{:S(2)}) async-start(), calls=%async_computation.1 | async-start | bytes 3145728 | tf_op jit(solution)/shard_map/reduce_scatter | solution.py:124
  72.2 227.1 %copy-start.14 = (s32[1024]{0:T(1024)}, s32[1024]{0:T(1024)S(1)}, u32[]{:S(2)}) copy-start(s32[1024]{0:T(1024)S(1)} %pad_clamp_fusion) | copy-start | bytes 12292
  302.6 4.3 copy-start
  306.9 2.7 copy-start.2
  309.6 1.2 copy-start.8
  310.8 22.2 %copy-start.9 = (f32[640,640]{1,0:T(8,128)S(1)}, f32[640,640]{1,0:T(8,128)}, u32[]{:S(2)}) copy-start(f32[640,640]{1,0:T(8,128)} %copy-done.8) | copy-start | bytes 4915204
  362.1 64.3 %copy-start.12 = (bf16[2,128]{1,0:T(2,128)(2,1)S(1)}, bf16[2,128]{1,0:T(2,128)(2,1)}, u32[]{:S(2)}) copy-start(bf16[2,128]{1,0:T(2,128)(2,1)} %param.6) | copy-start | bytes 1540
  423.0 11.3 %copy-start.5 = (f32[640,640]{1,0:T(8,128)}, f32[640,640]{1,0:T(8,128)S(1)}, u32[]{:S(2)}) copy-start(f32[640,640]{1,0:T(8,128)S(1)} %get-tuple-element.120) | copy-start | bytes 4915204
  432.9 1.4 copy-start.17
  617.5 3.4 copy-start.11
  636.1 2.9 copy-start.1
  636.1 2.9 copy-start.3
  642.5 2.2 copy-start.4
  645.0 1.2 copy-start.16
  649.0 237.8 %copy-start.15 = (pred[8]{0:T(512)(128)(4,1)S(1)}, pred[8]{0:T(512)(128)(4,1)}, u32[]{:S(2)}) copy-start(pred[8]{0:T(512)(128)(4,1)} %get-tuple-element.106) | copy-start | bytes 28
  649.0 237.8 %all-reduce.6.cloned.1.call-start = ((), (), s32[]{:S(2)}) async-start(), calls=%async_computation.2 | async-start | bytes 1048576 | tf_op jit(solution)/shard_map/psum | solution.py:131
  662.8 2.2 copy-start.10
  665.2 8.9 collective-permute-start.5
  665.8 9.0 %collective-permute-start.4 = (bf16[2,128,128]{2,0,1:T(2,128)(2,1)S(1)}, bf16[2,128,128]{2,0,1:T(2,128)(2,1)S(1)}, u32[]{:S(2)}, u32[]{:S(2)}) collective-permute-start(bf16[2,128,128]{2,0,1:T(2,128)(2,1)S(1)} %get-tuple-element.117), channel_id=1, source_target_pairs={{0,254},{2,0},{4,2},{6,4},{8,6},{10,8},{12,10},{14,12},{16,14},{18... | collective-permute-start | bytes 196616 | tf_op jit(solution)/shard_map/ppermute | solution.py:18
  (3 other events, 2.8 us)
Sparse Core Ops, SparseCore 0:
  70.0 219.9 all-reduce.7
  649.1 13.6 reduce-scatter.1
  669.1 217.6 all-reduce.5
where the time goes:
time: 904 us; the launch traced here: 897 us
  waiting for transfers between devices  443 us (49%)
  other arithmetic  265 us (29%)
  local copies, waits for them, and re-layouts  58.9 us (7%)
  matrix products  45.5 us (5%)
  between operations  40 us (4%)
  blocking collectives  28.7 us (3%)
  starting transfers between devices  15.1 us (2%)
    psum x1, waiting for transfers between devices, from_root(): return lax.psum(kept, axis)  217 us
    psum x1, waiting for transfers between devices, body(): hot_back = lax.psum(grad_half[3 * per_dev:], 'blk')  212 us
    another operation x20, other arithmetic, loglik_of(): chol = jnp.linalg.cholesky(sigma)  162 us
    another operation x4, other arithmetic, loglik_of(): solved = jax.scipy.linalg.solve_triangular(chol, joint_y, lower=True)  50.6 us
    scatter-add x1, other arithmetic, loglik_of(): logs = jnp.log(jnp.diagonal(chol)[joint - own:])  34.9 us
    pmax x1, blocking collectives, body(): marks = lax.pmax(marks, 'blk')  26.2 us
    another operation x30, local copies, waits for them, and re-layouts  23.8 us
    another operation x26, matrix products, loglik_of(): chol = jnp.linalg.cholesky(sigma)  19.2 us
  transfers between devices with their start and end apart: 9, of which 4 were waited for; matrix products, arithmetic and copies ran while one was open for 16% of the time, Pallas kernels for 0%

commit v1 on v0

v1 whole, which is shorter than its diff:
```python
import functools
import math

import jax
import jax.numpy as jnp
from jax import lax
from jax.experimental import pallas as pl
from jax.experimental.pallas import tpu as pltpu
from jax.sharding import PartitionSpec as P

HOT = 8
T = 128
G = 8
VMEM = pl.BlockSpec(memory_space=pltpu.VMEM)
HI = lax.Precision.HIGHEST


def dot32(a, b, dims=((1,), (0,))):
    return lax.dot_general(a, b, (dims, ((), ())), precision=HI, preferred_element_type=jnp.float32)


def negative_inverse(ref):
    lane = lax.broadcasted_iota(jnp.int32, (G, T), 1)
    sub = lax.broadcasted_iota(jnp.int32, (G, T), 0)

    def group(step, logs):
        a = ref[...]
        cols = [jnp.broadcast_to(a[:, k : k + 1], (T, T)) for k in range(G)]
        rows = []
        for k in range(G):
            row = jnp.broadcast_to(a[k : k + 1, :], (G, T))
            rows.append(jnp.where(lane < G, jnp.where(lane == k, -1.0, 0.0), row))
        s = {}
        for k in range(G):
            for i in range(k, G):
                s[i, k] = jnp.broadcast_to(cols[k][i : i + 1, :], (G, T))
        inv = []
        low = {}
        prod = None
        for k in range(G):
            d = s[k, k]
            prod = d if prod is None else prod * d
            r = 1.0 / d
            inv.append(r)
            for i in range(k + 1, G):
                low[i, k] = s[i, k] * r
            for i in range(k + 1, G):
                for m in range(k + 1, i + 1):
                    s[i, m] = s[i, m] - low[i, k] * s[m, k]
                rows[i] = rows[i] - low[i, k] * rows[k]
        for k in reversed(range(G)):
            x = rows[k] * inv[k]
            for i in range(k + 1, G):
                x = x - low[i, k] * rows[i]
            rows[k] = x
        top = rows[0]
        for k in range(1, G):
            top = jnp.where(sub == k, rows[k], top)
        for t in range(1, T // G):
            blk = jnp.where(lane < G, 0.0, a[t * G : (t + 1) * G, :])
            for k in range(G):
                blk = blk - cols[k][t * G : (t + 1) * G, :] * rows[k]
            ref[(t - 1) * G : t * G, :] = pltpu.roll(blk, T - G, 1)
        ref[T - G :, :] = pltpu.roll(top, T - G, 1)
        return logs + jnp.log(prod)

    return lax.fori_loop(0, T // G, group, jnp.zeros((G, T), jnp.float32))


def block_kernel(nb, slot_ref, mine_ref, other_ref, value_ref, gmine_ref, gother_ref, x_ref, kern, work, piv, right, ext):
    joint, width = x_ref.shape
    lead = joint - T
    for k in range(nb):
        rs = pl.ds(k * T, T)
        x_ref[rs, :T] = mine_ref[slot_ref[k], :T, :]
        x_ref[rs, T:] = other_ref[slot_ref[k], :T, :]
        obs = mine_ref[slot_ref[k], T:, :].astype(jnp.float32)[0:1, :]
        work[rs, joint:] = jnp.transpose(jnp.broadcast_to(obs, (T, T)))
    wide = x_ref[...].astype(jnp.float32)
    sq = jnp.sum(wide * wide, axis=1, keepdims=True)
    sq_row = jnp.transpose(jnp.broadcast_to(sq, (joint, T)))[0:1, :]
    col = lax.broadcasted_iota(jnp.int32, (T, joint), 1)
    row = lax.broadcasted_iota(jnp.int32, (T, joint), 0)
    for k in range(nb):
        rs = pl.ds(k * T, T)
        gram = lax.dot_general(
            x_ref[rs, :], x_ref[...], (((1,), (1,)), ((), ())), preferred_element_type=jnp.float32
        )
        dist = sq[k * T : (k + 1) * T] + sq_row - 2.0 * gram
        kr = jnp.where(col == row + k * T, 1.1, jnp.exp(-dist * (0.5 / width)))
        kern[rs, :] = kr
        work[rs, :joint] = kr
    for k in range(nb - 1):
        a, b = k * T, (k + 1) * T
        piv[...] = work[a:b, a:b]
        negative_inverse(piv)
        t = -dot32(piv[...], work[a:b, b:])
        work[b:, b:] = work[b:, b:] - dot32(work[b:, a:b], t)
        work[a:b, b:] = t
    right[lead - T :, :] = work[lead - T : lead, lead:]
    for k in reversed(range(nb - 2)):
        a, b = k * T, (k + 1) * T
        right[a:b, :] = work[a:b, lead:] - dot32(work[a:b, b:lead], right[b:, :])
    piv[...] = work[lead:, lead:joint]
    res = work[lead:, joint:]
    logs = negative_inverse(piv)
    sinv = -piv[...]
    u = dot32(sinv, res)
    quad = jnp.sum(res * u, axis=0, keepdims=True)
    value_ref[...] = -0.5 * (quad + logs) - 0.5 * T * math.log(2.0 * math.pi)
    inner = sinv - u * jnp.transpose(u)
    ident = jnp.where(
        lax.broadcasted_iota(jnp.int32, (T, T), 0) == lax.broadcasted_iota(jnp.int32, (T, T), 1), 1.0, 0.0
    )
    lane = lax.broadcasted_iota(jnp.int32, (T, T), 1)
    for k in range(nb):
        rs = slice(k * T, (k + 1) * T)
        e = -right[rs, :T] if k < nb - 1 else ident
        alpha = right[rs, T:] if k < nb - 1 else jnp.zeros((T, T), jnp.float32)
        v = dot32(e, u)
        ext[rs, :T] = e
        ext[rs, T:] = jnp.where(lane == 0, v, jnp.where(lane == 1, alpha, 0.0))
        work[rs, :T] = -dot32(e, inner)
        work[rs, T : 2 * T] = jnp.where(lane == 0, alpha, jnp.where(lane == 1, v, 0.0))
    gmine_ref[...] = jnp.zeros_like(gmine_ref)
    gother_ref[...] = jnp.zeros_like(gother_ref)
    for k in range(nb):
        rs = slice(k * T, (k + 1) * T)
        m = dot32(work[rs, : 2 * T], ext[...], ((1,), (1,)))
        sym = jnp.where(col == row + k * T, 0.0, m * kern[rs, :] * (-0.5 / width)).astype(jnp.bfloat16)
        rowsum = jnp.sum(sym.astype(jnp.float32), axis=1, keepdims=True)
        part = jnp.dot(sym, x_ref[...], preferred_element_type=jnp.float32)
        grad = 2.0 * (rowsum * x_ref[rs, :].astype(jnp.float32) - part)
        gmine_ref[slot_ref[k]] = grad[:, :T].astype(jnp.bfloat16)
        gother_ref[slot_ref[k]] = grad[:, T:].astype(jnp.bfloat16)


NX, NZ, NY = 4, 8, 4
NEAR = 2
OWN = 2
PACK = T + 16
NPOOL = OWN * (NEAR + 1) + HOT
MESH = pl.DeviceIdType.MESH


class Place:
    def __init__(self):
        self.blk = lax.axis_index("blk")
        self.rep = lax.axis_index("rep")
        self.x = self.blk % NX
        self.z = self.blk // NX % NZ
        self.y = self.blk // (NX * NZ)

    def along_x(self, by):
        return self.blk - self.x + (self.x + by) % NX, self.rep

    def along_z(self, by):
        return self.blk + ((self.z + by) % NZ - self.z) * NX, self.rep

    def along_y(self, by):
        return (self.blk + by * NX * NZ) % (NX * NZ * NY), self.rep

    def along_blk(self, by):
        return (self.blk + by) % (NX * NZ * NY), self.rep

    def partner(self):
        return self.blk, 1 - self.rep

    def greet(self):
        there = [self.along_z(o) for o in range(1, NZ)]
        there += [self.along_x(o) for o in range(1, NX)]
        there += [self.along_y(o) for o in range(1, NY)]
        there += [self.along_blk(o) for o in (1, 2, -1, -2)]
        there += [self.partner()]
        barrier = pltpu.get_barrier_semaphore()
        for device in there:
            pl.semaphore_signal(barrier, inc=1, device_id=device, device_id_type=MESH)
        pl.semaphore_wait(barrier, len(there))


def send(src, dst, sems, index, device):
    copy = pltpu.make_async_remote_copy(
        src_ref=src,
        dst_ref=dst,
        send_sem=sems.at[0, index],
        recv_sem=sems.at[1, index],
        device_id=device,
        device_id_type=MESH,
    )
    copy.start()
    return copy


def share(src, got, sems, where, count):
    copies = [send(src, got.at[o - 1], sems, o - 1, where(o)) for o in range(1, count)]
    for copy in copies:
        copy.wait()
    total = src[...].astype(jnp.float32)
    for o in range(1, count):
        total = total + got[o - 1].astype(jnp.float32)
    return total


def sum_slots(place, slots, result, zgot, xgot, ygot, held, zs, xs, ys, gs):
    z = place.z
    copies = []
    for o in range(1, NZ):
        copies.append(send(slots.at[(z + o) % NZ], zgot.at[o - 1], zs, o - 1, place.along_z(o)))
    for copy in copies:
        copy.wait()
    total = slots[z].astype(jnp.float32)
    for o in range(1, NZ):
        total = total + zgot[o - 1].astype(jnp.float32)
    held[0] = total.astype(held.dtype)
    total = share(held.at[0], xgot, xs, place.along_x, NX)
    held[1] = total.astype(held.dtype)
    total = share(held.at[1], ygot, ys, place.along_y, NY)
    held[2] = total.astype(held.dtype)
    copies = [send(held.at[2], result.at[z], gs, o - 1, place.along_z(o)) for o in range(1, NZ)]
    result[z] = held[2]
    for copy in copies:
        copy.wait()


def pick_weights(place, marks):
    ids = lax.broadcasted_iota(jnp.int32, (G, T), 0) * T + lax.broadcasted_iota(jnp.int32, (G, T), 1)
    named = jnp.where(marks > 0.5, 1.0, 0.0)
    weights = []
    for c in range(OWN):
        own = place.blk * OWN + c
        here = jnp.sum(jnp.where(ids == own, named, 0.0), keepdims=True)
        rank = jnp.sum(jnp.where(ids < own, named, 0.0), keepdims=True)
        weights.append([here * jnp.where(jnp.abs(rank - s) < 0.5, 1.0, 0.0) for s in range(HOT)])
    return weights


def gather_kernel(cond_ref, own_ref, pool_ref, other_ref, marks_ref, m0, m1, m2, mz, mx, my,
                  slots, hot, zgot, xgot, ygot, held, ms, ns, zs, xs, ys, gs, ps):
    place = Place()
    place.greet()
    near = []
    for by in (1, 2):
        near.append(send(own_ref, pool_ref.at[pl.ds(by * OWN, OWN)], ns, by - 1, place.along_blk(by)))
    ids = lax.broadcasted_iota(jnp.int32, (G, T), 0) * T + lax.broadcasted_iota(jnp.int32, (G, T), 1)
    marks = jnp.zeros((G, T), jnp.float32)
    for c in range(OWN):
        for k in (2, 3):
            marks = jnp.where(ids == cond_ref[c, k], 1.0, marks)
    m0[...] = marks
    pool_ref[:OWN] = own_ref[...]
    m1[...] = share(m0, mz, ms.at[:, pl.ds(0, NZ - 1)], place.along_z, NZ)
    m2[...] = share(m1, mx, ms.at[:, pl.ds(NZ - 1, NX - 1)], place.along_x, NX)
    marks = share(m2, my, ms.at[:, pl.ds(NZ + NX - 2, NY - 1)], place.along_y, NY)
    marks_ref[...] = marks
    weights = pick_weights(place, marks)
    for s in range(HOT):
        value = weights[0][s] * own_ref[0].astype(jnp.float32)
        for c in range(1, OWN):
            value = value + weights[c][s] * own_ref[c].astype(jnp.float32)
        slots[s] = value.astype(jnp.bfloat16)
    early = [send(own_ref, other_ref.at[pl.ds(0, OWN)], ps, 0, place.partner())]
    for by in (1, 2):
        near[by - 1].wait()
        part = pl.ds(by * OWN, OWN)
        early.append(send(pool_ref.at[part], other_ref.at[part], ps, by, place.partner()))
    sum_slots(place, slots, hot, zgot, xgot, ygot, held, zs, xs, ys, gs)
    part = pl.ds(OWN * (NEAR + 1), HOT)
    early.append(send(hot, other_ref.at[part], ps, NEAR + 1, place.partner()))
    pool_ref[part] = hot[...]
    for copy in early:
        copy.wait()


def return_kernel(marks_ref, mine_ref, theirs_ref, out_ref, got, near_out, near_got,
                  slots, hot, zgot, xgot, ygot, held, ns, zs, xs, ys, gs, ps):
    place = Place()
    place.greet()
    parts = [pl.ds(OWN * (NEAR + 1), HOT), pl.ds(0, OWN * (NEAR + 1))]
    copies = [send(theirs_ref.at[p], got.at[p], ps, i, place.partner()) for i, p in enumerate(parts)]
    copies[0].wait()
    part = parts[0]
    slots[...] = (mine_ref[part].astype(jnp.float32) + got[part].astype(jnp.float32)).astype(jnp.bfloat16)
    copies[1].wait()
    part = pl.ds(OWN, OWN * NEAR)
    near_out[...] = (mine_ref[part].astype(jnp.float32) + got[part].astype(jnp.float32)).astype(jnp.bfloat16)
    near = []
    for by in (1, 2):
        part = pl.ds((by - 1) * OWN, OWN)
        near.append(send(near_out.at[part], near_got.at[part], ns, by - 1, place.along_blk(-by)))
    sum_slots(place, slots, hot, zgot, xgot, ygot, held, zs, xs, ys, gs)
    weights = pick_weights(place, marks_ref[...])
    for copy in near:
        copy.wait()
    for c in range(OWN):
        total = mine_ref[c].astype(jnp.float32) + got[c].astype(jnp.float32)
        for by in range(NEAR):
            total = total + near_got[by * OWN + c].astype(jnp.float32)
        for s in range(HOT):
            total = total + weights[c][s] * hot[s].astype(jnp.float32)
        out_ref[c * T : (c + 1) * T, :] = total


def ring_scratch(rows):
    half = jnp.bfloat16
    return [
        pltpu.VMEM((HOT, rows, T), half),
        pltpu.VMEM((HOT, rows, T), half),
        pltpu.VMEM((NZ - 1, rows, T), half),
        pltpu.VMEM((NX - 1, rows, T), half),
        pltpu.VMEM((NY - 1, rows, T), half),
        pltpu.VMEM((3, rows, T), half),
    ]


def dma(count):
    return pltpu.SemaphoreType.DMA((2, count))


def ring_sems():
    return [dma(NEAR), dma(NZ - 1), dma(NX - 1), dma(NY - 1), dma(NZ - 1)]


def body(features, observations, cond_ids):
    per_dev = cond_ids.shape[0]
    ncond = cond_ids.shape[1]
    half = features.shape[1]
    joint = (ncond + 1) * T
    device = lax.axis_index("blk")
    core = lax.axis_index("rep")
    obs = jnp.broadcast_to(observations[:, None, :], (per_dev, PACK - T, T))
    own = jnp.concatenate([features.reshape(per_dev, T, half), obs], axis=1)
    small = pltpu.VMEM((G, T), jnp.float32)
    pool, other, marks = pl.pallas_call(
        gather_kernel,
        out_shape=(
            jax.ShapeDtypeStruct((NPOOL, PACK, T), jnp.bfloat16),
            jax.ShapeDtypeStruct((NPOOL, PACK, T), jnp.bfloat16),
            jax.ShapeDtypeStruct((G, T), jnp.float32),
        ),
        in_specs=[pl.BlockSpec(memory_space=pltpu.SMEM), VMEM],
        out_specs=(VMEM, VMEM, VMEM),
        scratch_shapes=[small] * 3
        + [pltpu.VMEM((n - 1, G, T), jnp.float32) for n in (NZ, NX, NY)]
        + ring_scratch(PACK)
        + [dma(NZ + NX + NY - 3)]
        + ring_sems()
        + [dma(NEAR + 2)],
        compiler_params=pltpu.CompilerParams(
            collective_id=0, has_side_effects=True, vmem_limit_bytes=30 << 20
        ),
        name="gather_blocks",
    )(cond_ids, own)
    named = (marks[:2].reshape(-1) > 0.5).astype(jnp.int32)
    mine = lax.dynamic_index_in_dim(cond_ids, core, 0, keepdims=False)
    near_ids = mine[:2]
    near_slots = (device - near_ids // OWN) % (NX * NZ * NY) * OWN + near_ids % OWN
    below = jnp.arange(named.shape[0], dtype=jnp.int32)[None, :] < mine[2:, None]
    hot_slots = OWN * (NEAR + 1) + jnp.sum(jnp.where(below, named[None, :], 0), axis=1)
    slots = jnp.concatenate([near_slots, hot_slots, core[None].astype(jnp.int32)])
    value, gmine, gother = pl.pallas_call(
        functools.partial(block_kernel, ncond + 1),
        out_shape=(
            jax.ShapeDtypeStruct((G, T), jnp.float32),
            jax.ShapeDtypeStruct((NPOOL, T, T), jnp.bfloat16),
            jax.ShapeDtypeStruct((NPOOL, T, T), jnp.bfloat16),
        ),
        in_specs=[pl.BlockSpec(memory_space=pltpu.SMEM), VMEM, VMEM],
        out_specs=(VMEM, VMEM, VMEM),
        scratch_shapes=[
            pltpu.VMEM((joint, 2 * T), jnp.bfloat16),
            pltpu.VMEM((joint, joint), jnp.float32),
            pltpu.VMEM((joint, joint + T), jnp.float32),
            pltpu.VMEM((T, T), jnp.float32),
            pltpu.VMEM((joint - T, 2 * T), jnp.float32),
            pltpu.VMEM((joint, 2 * T), jnp.float32),
        ],
        compiler_params=pltpu.CompilerParams(vmem_limit_bytes=40 << 20),
        name="block_terms",
    )(slots, pool, other)
    grad = pl.pallas_call(
        return_kernel,
        out_shape=jax.ShapeDtypeStruct((per_dev * T, half), jnp.float32),
        in_specs=[VMEM] * 3,
        out_specs=VMEM,
        scratch_shapes=[
            pltpu.VMEM((NPOOL, T, T), jnp.bfloat16),
            pltpu.VMEM((OWN * NEAR, T, T), jnp.bfloat16),
            pltpu.VMEM((OWN * NEAR, T, T), jnp.bfloat16),
        ]
        + ring_scratch(T)
        + ring_sems()
        + [dma(2)],
        compiler_params=pltpu.CompilerParams(
            collective_id=1, has_side_effects=True, vmem_limit_bytes=30 << 20
        ),
        name="return_gradients",
    )(marks, gmine, gother)
    return (value[0, :1], grad)


def solution(mesh):
    placed = (P("blk", "rep"), P("blk", None), P("blk", None))
    return jax.shard_map(
        body,
        mesh=mesh,
        in_specs=placed,
        out_specs=(P(("blk", "rep")), P("blk", "rep")),
        check_vma=False,
    )
```

time: 904 us -> 126 us (0.14)
  waiting for transfers between devices: 443 us -> 0 us
  other arithmetic: 265 us -> 1.13 us
  Pallas kernels: 0 us -> 122 us
  local copies, waits for them, and re-layouts: 58.9 us -> 2.51 us
  matrix products: 45.5 us -> 0 us
  between operations: 40 us -> 0.68 us
  blocking collectives: 28.7 us -> 0 us
  starting transfers between devices: 15.1 us -> 0 us
    psum x2 -> x0, waiting for transfers between devices: 429 us -> none  [the longest x1 217 us: from_root(): return lax.psum(kept, axis)]
    another operation x25 -> x0, other arithmetic: 212 us -> none  [the longest x20 162 us: loglik_of(): chol = jnp.linalg.cholesky(sigma)]
    pallas_call x0 -> x3, Pallas kernels: none -> 122 us  [the longest x1 46.7 us: body(): pl.pallas_call(gather_kernel, out_shape=(jax.ShapeDtypeStruct((NPOOL, PAC...]
    scatter-add x1 -> x0, other arithmetic: 34.9 us -> none  [loglik_of(): logs = jnp.log(jnp.diagonal(chol)[joint - own:])]
    another operation x44 -> x0, matrix products: 30.9 us -> none  [the longest x26 19.2 us: loglik_of(): chol = jnp.linalg.cholesky(sigma)]
    another operation x41 -> x0, local copies, waits for them, and re-layouts: 26.3 us -> none
    pmax x1 -> x0, blocking collectives: 26.2 us -> none  [body(): marks = lax.pmax(marks, 'blk')]
    ppermute x6 -> x0, starting transfers between devices: 15 us -> none  [from_behind(): lax.ppermute(array, axis, [(i, (i + by) % length) for i in range(length)])]
  transfers between devices with their start and end apart: 9 -> 0, of which waited for: 4 -> 0; matrix products, arithmetic and copies ran while one was open for 16% -> 0% of each run, Pallas kernels for 0% -> 0%
where the time goes in v1:
time: 126 us
  Pallas kernels  122 us (97%)
  local copies, waits for them, and re-layouts  2.51 us (2%)
    pallas_call x1, Pallas kernels, body(): pl.pallas_call(gather_kernel, out_shape=(jax.ShapeDtypeStruct((NPOOL, PAC...  46.7 us
    pallas_call x1, Pallas kernels, body(): pl.pallas_call(functools.partial(block_kernel, ncond + 1), out_shape=(jax...  43.4 us
    pallas_call x1, Pallas kernels, body(): pl.pallas_call(return_kernel, out_shape=jax.ShapeDtypeStruct((per_dev * T...  31.5 us

profile of v1, /device:TPU:4, one launch (start us, length us, event | category | flops | bytes accessed | tf_op | source)
XLA Modules:
  0.0 125.9 jit_solution(2719552964490590610)
XLA Ops:
  0.6 0.0 copy-start
  0.6 0.7 copy-done
  1.3 0.0 copy-start.1
  1.3 0.1 slice_bitcast_fusion
  1.4 0.6 copy-done.1
  2.0 0.8 pad_maximum_fusion.own_ref
  2.8 46.7 %gather_blocks.1 = (bf16[14,144,128]{2,1,0:T(8,128)(2,1)S(1)}, bf16[14,144,128]{2,1,0:T(8,128)(2,1)S(1)}, f32[8,128]{1,0:T(8,128)S(1)}) custom-call(s32[2,4]{1,0:T(2,128)S(1)} %copy-done, bf16[2,144,128]{2,1,0:T(8,128)(2,1)S(1)} %pad_maximum_fusion.own_ref), custom_call_target="tpu_custom_call" | custom-call | tf_op jit(solution)/shard_map/gather_blocks/pallas_call | solution.py:333
  49.5 0.2 fusion
  49.7 0.1 pad_add_fusion.slot_ref
  49.8 43.4 %block_terms.1 = (f32[8,128]{1,0:T(8,128)S(1)}, bf16[14,128,128]{2,1,0:T(8,128)(2,1)S(1)}, bf16[14,128,128]{2,1,0:T(8,128)(2,1)S(1)}) custom-call(s32[5]{0:T(128)S(1)} %pad_add_fusion.slot_ref, bf16[14,144,128]{2,1,0:T(8,128)(2,1)S(1)} %get-tuple-element.9.mine_ref, bf16[14,144,128]{2,1,0:T(8,128)(2,1)S(1)} %get-tuple-element.10.other_ref), custom_call_target="tpu_custom_call" | custom-call | tf_op jit(solution)/shard_map/block_terms/pallas_call | solution.py:360
  93.2 0.5 slice.20
  93.8 31.5 %return_gradients.1 = f32[256,128]{1,0:T(8,128)S(1)} custom-call(f32[8,128]{1,0:T(8,128)S(1)} %get-tuple-element.8.marks_ref, bf16[14,128,128]{2,1,0:T(8,128)(2,1)S(1)} %get-tuple-element.12.mine_ref, bf16[14,128,128]{2,1,0:T(8,128)(2,1)S(1)} %get-tuple-element.13.theirs_ref), custom_call_target="tpu_custom_call" | custom-call | tf_op jit(solution)/shard_map/return_gradients/pallas_call | solution.py:380
  125.2 0.7 copy.6
  (4 shorter events, 0.0 us)
Async XLA Ops:
  0.6 0.7 copy-start
  1.3 0.7 copy-start.1

commit v2 on v0

v2 whole, which is shorter than its diff:
```python
import math

import jax
import jax.numpy as jnp
from jax import lax
from jax.experimental import pallas as pl
from jax.experimental.pallas import tpu as pltpu
from jax.sharding import PartitionSpec as P

HOT = 8
T = 128
G = 8
VMEM = pl.BlockSpec(memory_space=pltpu.VMEM)
HI = lax.Precision.HIGHEST


def dot32(a, b, dims=((1,), (0,))):
    return lax.dot_general(a, b, (dims, ((), ())), precision=HI, preferred_element_type=jnp.float32)


UNROLL = 8


def add_up(terms):
    while len(terms) > 1:
        odd = terms[-1:] if len(terms) % 2 else []
        terms = [a + b for a, b in zip(terms[::2], terms[1::2])] + odd
    return terms[0]


def invert_rows(rows, s):
    prod = None
    inv = {}
    for k in range(0, G, 2):
        j = k + 1
        a, b, c = s[k, k], s[j, k], s[j, j]
        det = a * c - b * b
        prod = det if prod is None else prod * det
        r = 1.0 / det
        ra, rb, rc = a * r, b * r, c * r
        inv[k] = (ra, rb, rc)
        rest = [i for i in range(G) if i not in (k, j)]
        low = {}
        for m in range(j + 1, G):
            s[k, m], s[j, m] = s[m, k], s[m, j]
        for i in rest:
            p, q = s[i, k], s[i, j]
            low[i] = (p * rc - q * rb, q * ra - p * rb)
        for i in rest:
            for m in range(j + 1, G):
                if i < k or i >= m:
                    sk, sj = s[m, k], s[m, j]
                    s[i, m] = s[i, m] - (low[i][0] * sk + low[i][1] * sj)
        for i in rest:
            rows[i] = rows[i] - (low[i][0] * rows[k] + low[i][1] * rows[j])
    for k in range(0, G, 2):
        ra, rb, rc = inv[k]
        x, y = rows[k], rows[k + 1]
        rows[k], rows[k + 1] = rc * x - rb * y, ra * y - rb * x
    return prod


def negative_inverse(ref):
    lane = lax.broadcasted_iota(jnp.int32, (G, T), 1)
    sub = lax.broadcasted_iota(jnp.int32, (G, T), 0)
    count = T // G

    def groups(step, logs):
        blks = [ref[t * G : (t + 1) * G, :] for t in range(count)]
        for u in range(UNROLL):
            first = u * G
            inside = (lane >= first) & (lane < first + G)
            panel = blks[u]
            rows = []
            for k in range(G):
                row = jnp.broadcast_to(panel[k : k + 1, :], (G, T))
                rows.append(jnp.where(inside, jnp.where(lane == first + k, -1.0, 0.0), row))
            s = {}
            for k in range(G):
                col = jnp.broadcast_to(panel[:, first + k : first + k + 1], (G, T))
                for i in range(k, G):
                    s[i, k] = jnp.broadcast_to(col[i : i + 1, :], (G, T))
                    s[k, i] = s[i, k]
            prod = invert_rows(rows, s)
            logs = logs + jnp.log(prod)
            order = [(u + d) % count for d in range(1, count)]
            for t in order:
                old = blks[t]
                terms = [
                    jnp.broadcast_to(old[:, first + k : first + k + 1], (G, T)) * rows[k] for k in range(G)
                ]
                blks[t] = jnp.where(inside, 0.0, old) - add_up(terms)
            top = rows[0]
            for k in range(1, G):
                top = jnp.where(sub == k, rows[k], top)
            blks[u] = top
        shift = UNROLL * G
        for t in range(count):
            at = (t - UNROLL) % count
            ref[at * G : (at + 1) * G, :] = blks[t] if shift == T else pltpu.roll(blks[t], T - shift, 1)
        return logs

    zero = jnp.zeros((G, T), jnp.float32)
    if UNROLL == count:
        return groups(0, zero)
    return lax.fori_loop(0, count // UNROLL, groups, zero)


NX, NZ, NY = 4, 8, 4
NEAR = 2
OWN = 2
PACK = T + 16
MESH = pl.DeviceIdType.MESH


class Place:
    def __init__(self):
        self.blk = lax.axis_index("blk")
        self.rep = lax.axis_index("rep")
        self.x = self.blk % NX
        self.z = self.blk // NX % NZ
        self.y = self.blk // (NX * NZ)

    def along_x(self, by):
        return self.blk - self.x + (self.x + by) % NX, self.rep

    def along_z(self, by):
        return self.blk + ((self.z + by) % NZ - self.z) * NX, self.rep

    def along_y(self, by):
        return (self.blk + by * NX * NZ) % (NX * NZ * NY), self.rep

    def along_blk(self, by):
        return (self.blk + by) % (NX * NZ * NY), self.rep

    def partner(self):
        return self.blk, 1 - self.rep

    def greet(self):
        there = [self.along_z(o) for o in range(1, NZ)]
        there += [self.along_x(o) for o in range(1, NX)]
        there += [self.along_y(o) for o in range(1, NY)]
        there += [self.along_blk(o) for o in (1, 2, -1, -2)]
        there += [self.partner()]
        barrier = pltpu.get_barrier_semaphore()
        for device in there:
            pl.semaphore_signal(barrier, inc=1, device_id=device, device_id_type=MESH)
        pl.semaphore_wait(barrier, len(there))


def send(src, dst, sems, index, device):
    copy = pltpu.make_async_remote_copy(
        src_ref=src,
        dst_ref=dst,
        send_sem=sems.at[0, index],
        recv_sem=sems.at[1, index],
        device_id=device,
        device_id_type=MESH,
    )
    copy.start()
    return copy


def pick_weights(place, marks):
    ids = lax.broadcasted_iota(jnp.int32, (G, T), 0) * T + lax.broadcasted_iota(jnp.int32, (G, T), 1)
    named = jnp.where(marks > 0.5, 1.0, 0.0)
    weights = []
    for c in range(OWN):
        own = place.blk * OWN + c
        here = jnp.sum(jnp.where(ids == own, named, 0.0), keepdims=True)
        rank = jnp.sum(jnp.where(ids < own, named, 0.0), keepdims=True)
        weights.append([here * jnp.where(jnp.abs(rank - s) < 0.5, 1.0, 0.0) for s in range(HOT)])
    return weights


def start_stage(src, got, sems, where, count):
    return [send(src, got.at[o - 1], sems, o - 1, where(o)) for o in range(1, count)]


def end_stage(copies, mine, got):
    for copy in copies:
        copy.wait()
    return add_up([mine.astype(jnp.float32)] + [got[o].astype(jnp.float32) for o in range(len(copies))])


def start_scatter(place, slots, got, sems):
    return [
        send(slots.at[(place.z + o) % NZ], got.at[o - 1], sems, o - 1, place.along_z(o)) for o in range(1, NZ)
    ]


def start_gather(place, mine, result, sems):
    copies = [send(mine, result.at[place.z], sems, o - 1, place.along_z(o)) for o in range(1, NZ)]
    result[place.z] = mine[...]
    return copies


def weighted(weights, values):
    return add_up([w * v.astype(jnp.float32) for w, v in zip(weights, values)])


class Terms:
    def __init__(self, x, kern, work, piv, inverse, right, ext, squares):
        self.x, self.kern, self.work, self.piv, self.inverse = x, kern, work, piv, inverse
        self.right, self.ext, self.squares = right, ext, squares
        self.joint, self.width = x.shape
        self.lead = self.joint - T

    def place_rows(self, k, mine, other):
        rs = slice(k * T, (k + 1) * T)
        self.x[rs, :T] = mine[:T].astype(jnp.bfloat16)
        self.x[rs, T:] = other[:T].astype(jnp.bfloat16)
        obs = jnp.broadcast_to(mine[T : T + 1], (T, T))
        self.work[rs, self.joint :] = jnp.transpose(obs)
        wide = self.x[rs, :].astype(jnp.float32)
        self.squares[rs, :] = jnp.broadcast_to(jnp.sum(wide * wide, axis=1, keepdims=True), (T, T))

    def covariance(self, rows, cols):
        start, stop = cols
        for k in rows:
            rs = slice(k * T, (k + 1) * T)
            gram = lax.dot_general(
                self.x[rs, :],
                self.x[start * T : stop * T, :],
                (((1,), (1,)), ((), ())),
                preferred_element_type=jnp.float32,
            )
            for m in range(start, stop):
                across = jnp.transpose(self.squares[m * T : (m + 1) * T, :])
                dist = self.squares[rs, :] + across - 2.0 * gram[:, (m - start) * T : (m - start + 1) * T]
                kern = jnp.exp(-dist * (0.5 / self.width))
                if m == k:
                    kern = jnp.where(diagonal(), 1.1, kern)
                self.kern[rs, m * T : (m + 1) * T] = kern
                self.work[rs, m * T : (m + 1) * T] = kern

    def near_first(self):
        for rows, cols in (((0, 1, 4), (0, 2)), ((0, 1, 4), (4, 5))):
            self.covariance(rows, cols)
        self.piv[...] = self.work[:T, :T]

    def near_pivot(self, k):
        w = self.work
        a, b = k * T, (k + 1) * T
        negative_inverse(self.piv)
        minv = -self.piv[...]
        self.inverse[k] = minv
        groups = [(self.lead, self.joint + T)]
        if k == 0:
            groups.append((T, 2 * T))
        for lo, hi in groups:
            t = dot32(minv, w[a:b, lo:hi])
            w[a:b, lo:hi] = t
            for r in range(k + 1, 2):
                w[r * T : (r + 1) * T, lo:hi] = w[r * T : (r + 1) * T, lo:hi] - dot32(w[r * T : (r + 1) * T, a:b], t)
            w[self.lead :, lo:hi] = w[self.lead :, lo:hi] - dot32(w[self.lead :, a:b], t)
        if k == 0:
            self.piv[...] = w[T : 2 * T, T : 2 * T]

    def finish(self):
        w, joint, lead = self.work, self.joint, self.lead
        self.covariance((2, 3), (0, 5))
        self.covariance((0, 1, 4), (2, 4))
        hot = slice(2 * T, lead)
        first = dot32(self.inverse[0], w[:T, hot])
        w[:T, hot] = first
        w[T:, hot] = w[T:, hot] - dot32(w[T:, :T], first)
        w[hot, T : 2 * T] = w[hot, T : 2 * T] - dot32(w[hot, :T], w[:T, T : 2 * T])
        w[hot, lead:] = w[hot, lead:] - dot32(w[hot, :T], w[:T, lead:])
        second = dot32(self.inverse[1], w[T : 2 * T, hot])
        w[T : 2 * T, hot] = second
        w[2 * T :, hot] = w[2 * T :, hot] - dot32(w[2 * T :, T : 2 * T], second)
        w[hot, lead:] = w[hot, lead:] - dot32(w[hot, T : 2 * T], w[T : 2 * T, lead:])
        for k in (2, 3):
            a, b = k * T, (k + 1) * T
            self.piv[...] = w[a:b, a:b]
            negative_inverse(self.piv)
            t = -dot32(self.piv[...], w[a:b, b:])
            w[b:, b:] = w[b:, b:] - dot32(w[b:, a:b], t)
            w[a:b, b:] = t
        right = self.right
        right[lead - T :, :] = w[lead - T : lead, lead:]
        for k in (2, 1, 0):
            a, b = k * T, (k + 1) * T
            right[a:b, :] = w[a:b, lead:] - dot32(w[a:b, b:lead], right[b:, :])
        self.piv[...] = w[lead:, lead:joint]
        res = w[lead:, joint:]
        logs = negative_inverse(self.piv)
        sinv = -self.piv[...]
        u = dot32(sinv, res)
        quad = jnp.sum(res * u, axis=0, keepdims=True)
        inner = sinv - u * jnp.transpose(u)
        lane = lax.broadcasted_iota(jnp.int32, (T, T), 1)
        for k in range(5):
            rs = slice(k * T, (k + 1) * T)
            e = -right[rs, :T] if k < 4 else jnp.where(diagonal(), 1.0, 0.0)
            alpha = right[rs, T:] if k < 4 else jnp.zeros((T, T), jnp.float32)
            v = dot32(e, u)
            self.ext[rs, :T] = e
            self.ext[rs, T:] = jnp.where(lane == 0, v, jnp.where(lane == 1, alpha, 0.0))
            w[rs, :T] = -dot32(e, inner)
            w[rs, T : 2 * T] = jnp.where(lane == 0, alpha, jnp.where(lane == 1, v, 0.0))
        return -0.5 * (quad + logs) - 0.5 * T * math.log(2.0 * math.pi)

    def grad_rows(self, k):
        rs = slice(k * T, (k + 1) * T)
        col = lax.broadcasted_iota(jnp.int32, (T, self.joint), 1)
        row = lax.broadcasted_iota(jnp.int32, (T, self.joint), 0)
        m = dot32(self.work[rs, : 2 * T], self.ext[...], ((1,), (1,)))
        sym = jnp.where(col == row + k * T, 0.0, m * self.kern[rs, :] * (-0.5 / self.width)).astype(jnp.bfloat16)
        rowsum = jnp.sum(sym.astype(jnp.float32), axis=1, keepdims=True)
        part = jnp.dot(sym, self.x[...], preferred_element_type=jnp.float32)
        return 2.0 * (rowsum * self.x[rs, :].astype(jnp.float32) - part)


def diagonal():
    return lax.broadcasted_iota(jnp.int32, (T, T), 0) == lax.broadcasted_iota(jnp.int32, (T, T), 1)


def whole_kernel(cond_ref, own_ref, value_ref, out_ref,
                 m0, m1, m2, mz, mx, my,
                 near_mine, near_other, hot_mine, hot_other, slots, zgot, xgot, ygot, held,
                 x, kern, work, piv, inverse, right, ext, squares,
                 back_mine, back_other, back_got, side_mine, side_other, side_got, near_out, near_got,
                 slots2, hot2, zgot2, xgot2, ygot2, held2,
                 msem, nsem, psem, zsem, xsem, ysem, gsem, fsem,
                 nsem2, psem2, zsem2, xsem2, ysem2, gsem2):
    place = Place()
    terms = Terms(x, kern, work, piv, inverse, right, ext, squares)
    place.greet()
    ids = lax.broadcasted_iota(jnp.int32, (G, T), 0) * T + lax.broadcasted_iota(jnp.int32, (G, T), 1)
    marks = jnp.zeros((G, T), jnp.float32)
    for c in range(OWN):
        for k in (2, 3):
            marks = jnp.where(ids == cond_ref[c, k], 1.0, marks)
    m0[...] = marks
    stage = start_stage(m0, mz, msem.at[:, pl.ds(0, NZ - 1)], place.along_z, NZ)
    near = []
    for by in (1, 2):
        near.append(send(own_ref, near_mine.at[pl.ds(by * OWN, OWN)], nsem, by - 1, place.along_blk(by)))
    early = [send(own_ref, near_other.at[pl.ds(0, OWN)], psem, 0, place.partner())]
    near_mine[:OWN] = own_ref[...]
    m1[...] = end_stage(stage, m0[...], mz)
    stage = start_stage(m1, mx, msem.at[:, pl.ds(NZ - 1, NX - 1)], place.along_x, NX)
    for by in (1, 2):
        near[by - 1].wait()
        part = pl.ds(by * OWN, OWN)
        early.append(send(near_mine.at[part], near_other.at[part], psem, by, place.partner()))
    m2[...] = end_stage(stage, m1[...], mx)
    stage = start_stage(m2, my, msem.at[:, pl.ds(NZ + NX - 2, NY - 1)], place.along_y, NY)
    marks = end_stage(stage, m2[...], my)
    picks = pick_weights(place, marks)
    for s in range(HOT):
        slots[s] = weighted([p[s] for p in picks], [own_ref[c] for c in range(OWN)]).astype(jnp.bfloat16)
    stage = start_scatter(place, slots, zgot, zsem)
    for copy in early:
        copy.wait()
    near_ids = []
    for s in range(OWN * (NEAR + 1)):
        near_ids.append((place.blk + NX * NZ * NY - s // OWN) % (NX * NZ * NY) * OWN + s % OWN)
    near_w = [[jnp.where(cond_ref[place.rep, k] == i, 1.0, 0.0) for i in near_ids] for k in range(2)]
    own_w = [jnp.where(place.rep == c, 1.0, 0.0) for c in range(OWN)]
    count = len(near_ids)
    for k in range(2):
        terms.place_rows(
            k,
            weighted(near_w[k], [near_mine[s] for s in range(count)]),
            weighted(near_w[k], [near_other[s] for s in range(count)]),
        )
    terms.place_rows(
        4,
        weighted(own_w, [near_mine[c] for c in range(OWN)]),
        weighted(own_w, [near_other[c] for c in range(OWN)]),
    )
    terms.near_first()
    terms.near_pivot(0)
    held[0] = end_stage(stage, slots[place.z], zgot).astype(held.dtype)
    stage = start_stage(held.at[0], xgot, xsem, place.along_x, NX)
    held[1] = end_stage(stage, held[0], xgot).astype(held.dtype)
    stage = start_stage(held.at[1], ygot, ysem, place.along_y, NY)
    held[2] = end_stage(stage, held[1], ygot).astype(held.dtype)
    stage = start_gather(place, held.at[2], hot_mine, gsem)
    passed = [send(held.at[2], hot_other.at[place.z], fsem, 0, place.partner())]
    terms.near_pivot(1)
    for o in range(1, NZ):
        stage[o - 1].wait()
        slot = (place.z + NZ - o) % NZ
        passed.append(send(hot_mine.at[slot], hot_other.at[slot], fsem, o, place.partner()))
    named = jnp.where(marks > 0.5, 1.0, 0.0)
    hot_w = []
    for k in (2, 3):
        rank = jnp.sum(jnp.where(ids < cond_ref[place.rep, k], named, 0.0), keepdims=True)
        hot_w.append([jnp.where(jnp.abs(rank - s) < 0.5, 1.0, 0.0) for s in range(HOT)])
    mine = [weighted(w, [hot_mine[s] for s in range(HOT)]) for w in hot_w]
    for copy in passed:
        copy.wait()
    for k in (0, 1):
        terms.place_rows(2 + k, mine[k], weighted(hot_w[k], [hot_other[s] for s in range(HOT)]))
    value_ref[...] = terms.finish()
    grads = [terms.grad_rows(k) for k in (2, 3)]
    for s in range(HOT):
        total = weighted([w[s] for w in hot_w], grads).astype(jnp.bfloat16)
        back_mine[s] = total[:, :T]
        back_other[s] = total[:, T:]
    hot_copy = send(back_other, back_got, psem2, 0, place.partner())
    grads = [terms.grad_rows(k) for k in (0, 1, 4)]
    for s in range(count):
        weights = [near_w[0][s], near_w[1][s]] + ([own_w[s]] if s < OWN else [])
        total = weighted(weights, grads).astype(jnp.bfloat16)
        side_mine[s] = total[:, :T]
        side_other[s] = total[:, T:]
    side_copy = send(side_other, side_got, psem2, 1, place.partner())
    hot_copy.wait()
    slots2[...] = (back_mine[...].astype(jnp.float32) + back_got[...].astype(jnp.float32)).astype(jnp.bfloat16)
    stage = start_scatter(place, slots2, zgot2, zsem2)
    side_copy.wait()
    part = pl.ds(OWN, OWN * NEAR)
    near_out[...] = (side_mine[part].astype(jnp.float32) + side_got[part].astype(jnp.float32)).astype(jnp.bfloat16)
    near = []
    for by in (1, 2):
        part = pl.ds((by - 1) * OWN, OWN)
        near.append(send(near_out.at[part], near_got.at[part], nsem2, by - 1, place.along_blk(-by)))
    held2[0] = end_stage(stage, slots2[place.z], zgot2).astype(held2.dtype)
    stage = start_stage(held2.at[0], xgot2, xsem2, place.along_x, NX)
    held2[1] = end_stage(stage, held2[0], xgot2).astype(held2.dtype)
    stage = start_stage(held2.at[1], ygot2, ysem2, place.along_y, NY)
    held2[2] = end_stage(stage, held2[1], ygot2).astype(held2.dtype)
    stage = start_gather(place, held2.at[2], hot2, gsem2)
    for copy in near:
        copy.wait()
    for c in range(OWN):
        total = side_mine[c].astype(jnp.float32) + side_got[c].astype(jnp.float32)
        for by in range(NEAR):
            total = total + near_got[by * OWN + c].astype(jnp.float32)
        out_ref[c * T : (c + 1) * T, :] = total
    for copy in stage:
        copy.wait()
    for c in range(OWN):
        rs = slice(c * T, (c + 1) * T)
        out_ref[rs, :] = out_ref[rs, :] + weighted(picks[c], [hot2[s] for s in range(HOT)])


def half(*shape):
    return pltpu.VMEM(shape, jnp.bfloat16)


def full(*shape):
    return pltpu.VMEM(shape, jnp.float32)


def dma(count):
    return pltpu.SemaphoreType.DMA((2, count))


def body(features, observations, cond_ids):
    per_dev = cond_ids.shape[0]
    width = features.shape[1]
    joint = (cond_ids.shape[1] + 1) * T
    count = OWN * (NEAR + 1)
    obs = jnp.broadcast_to(observations[:, None, :], (per_dev, PACK - T, T))
    own = jnp.concatenate([features.reshape(per_dev, T, width), obs], axis=1)
    ring = [NZ - 1, NX - 1, NY - 1]
    value, grad = pl.pallas_call(
        whole_kernel,
        out_shape=(
            jax.ShapeDtypeStruct((G, T), jnp.float32),
            jax.ShapeDtypeStruct((per_dev * T, width), jnp.float32),
        ),
        in_specs=[pl.BlockSpec(memory_space=pltpu.SMEM), VMEM],
        out_specs=(VMEM, VMEM),
        scratch_shapes=[full(G, T)] * 3
        + [full(n, G, T) for n in ring]
        + [half(count, PACK, T)] * 2
        + [half(HOT, PACK, T)] * 3
        + [half(n, PACK, T) for n in ring + [3]]
        + [
            half(joint, 2 * T),
            full(joint, joint),
            full(joint, joint + T),
            full(T, T),
            full(2, T, T),
            full(joint - T, 2 * T),
            full(joint, 2 * T),
            full(joint, T),
        ]
        + [half(HOT, T, T)] * 3
        + [half(count, T, T)] * 3
        + [half(OWN * NEAR, T, T)] * 2
        + [half(HOT, T, T)] * 2
        + [half(n, T, T) for n in ring + [3]]
        + [dma(n) for n in (sum(ring), NEAR, NEAR + 1, *ring, NZ - 1, NZ)]
        + [dma(n) for n in (NEAR, 2, *ring, NZ - 1)],
        compiler_params=pltpu.CompilerParams(
            collective_id=0, has_side_effects=True, vmem_limit_bytes=50 << 20
        ),
        name="block_vecchia",
    )(cond_ids, own)
    return (value[0, :1], grad)


def solution(mesh):
    placed = (P("blk", "rep"), P("blk", None), P("blk", None))
    return jax.shard_map(
        body,
        mesh=mesh,
        in_specs=placed,
        out_specs=(P(("blk", "rep")), P("blk", "rep")),
        check_vma=False,
    )
```

time: 904 us -> 98.2 us (0.11)
  waiting for transfers between devices: 443 us -> 0 us
  other arithmetic: 265 us -> 0.86 us
  Pallas kernels: 0 us -> 94 us
  local copies, waits for them, and re-layouts: 58.9 us -> 1.82 us
  matrix products: 45.5 us -> 0 us
  between operations: 40 us -> 0.65 us
  blocking collectives: 28.7 us -> 0 us
  starting transfers between devices: 15.1 us -> 0 us
    psum x2 -> x0, waiting for transfers between devices: 429 us -> none  [the longest x1 217 us: from_root(): return lax.psum(kept, axis)]
    another operation x25 -> x0, other arithmetic: 212 us -> none  [the longest x20 162 us: loglik_of(): chol = jnp.linalg.cholesky(sigma)]
    pallas_call x0 -> x1, Pallas kernels: none -> 94 us  [body(): pl.pallas_call(whole_kernel, out_shape=(jax.ShapeDtypeStruct((G, T), jnp....]
    scatter-add x1 -> x0, other arithmetic: 34.9 us -> none  [loglik_of(): logs = jnp.log(jnp.diagonal(chol)[joint - own:])]
    another operation x44 -> x0, matrix products: 30.9 us -> none  [the longest x26 19.2 us: loglik_of(): chol = jnp.linalg.cholesky(sigma)]
    another operation x41 -> x0, local copies, waits for them, and re-layouts: 26.3 us -> none
    pmax x1 -> x0, blocking collectives: 26.2 us -> none  [body(): marks = lax.pmax(marks, 'blk')]
    ppermute x6 -> x0, starting transfers between devices: 15 us -> none  [from_behind(): lax.ppermute(array, axis, [(i, (i + by) % length) for i in range(length)])]
  transfers between devices with their start and end apart: 9 -> 0, of which waited for: 4 -> 0; matrix products, arithmetic and copies ran while one was open for 16% -> 0% of each run, Pallas kernels for 0% -> 0%
where the time goes in v2:
time: 98.2 us; the launch traced here: 97.3 us
  Pallas kernels  94 us (96%)
  local copies, waits for them, and re-layouts  1.82 us (2%)
    pallas_call x1, Pallas kernels, body(): pl.pallas_call(whole_kernel, out_shape=(jax.ShapeDtypeStruct((G, T), jnp....  94 us

profile of v2, /device:TPU:4, one launch (start us, length us, event | category | flops | bytes accessed | tf_op | source)
XLA Modules:
  0.0 97.3 jit_solution(15777488282572270327)
XLA Ops:
  0.6 0.0 copy-start.1
  0.6 0.6 copy-done.1
  1.3 0.0 copy-start
  1.3 0.9 pad_maximum_fusion.own_ref
  2.2 0.0 copy-done
  2.2 94.0 %block_vecchia.1 = (f32[8,128]{1,0:T(8,128)S(1)}, f32[256,128]{1,0:T(8,128)S(1)}) custom-call(s32[2,4]{1,0:T(2,128)S(1)} %copy-done, bf16[2,144,128]{2,1,0:T(8,128)(2,1)S(1)} %pad_maximum_fusion.own_ref), custom_call_target="tpu_custom_call" | custom-call | tf_op jit(solution)/shard_map/block_vecchia/pallas_call | solution.py:463
  96.2 0.5 slice.3
  96.7 0.7 copy.6
  (1 shorter events, 0.0 us)
Async XLA Ops:
  0.6 0.7 copy-start.1
  1.3 0.9 copy-start

commit v3 on v2

--- a/solution.py
+++ b/solution.py
@@ -19,6 +19,11 @@
 
 
 UNROLL = 8
+
+
+def split(value):
+    high = value.astype(jnp.bfloat16)
+    return high, (value - high.astype(jnp.float32)).astype(jnp.bfloat16)
 
 
 def add_up(terms):
@@ -60,7 +65,7 @@
     return prod
 
 
-def negative_inverse(ref):
+def negative_inverse(ref, half=False):
     lane = lax.broadcasted_iota(jnp.int32, (G, T), 1)
     sub = lax.broadcasted_iota(jnp.int32, (G, T), 0)
     count = T // G
@@ -100,10 +105,8 @@
             ref[at * G : (at + 1) * G, :] = blks[t] if shift == T else pltpu.roll(blks[t], T - shift, 1)
         return logs
 
-    zero = jnp.zeros((G, T), jnp.float32)
-    if UNROLL == count:
-        return groups(0, zero)
-    return lax.fori_loop(0, count // UNROLL, groups, zero)
+    steps = count // UNROLL
+    return lax.fori_loop(0, steps // 2 if half else steps, groups, jnp.zeros((G, T), jnp.float32))
 
 
 NX, NZ, NY = 4, 8, 4
@@ -127,6 +130,10 @@
     def along_z(self, by):
         return self.blk + ((self.z + by) % NZ - self.z) * NX, self.rep
 
+    def along_xy(self, by):
+        x, y = by % NX, by // NX
+        return ((self.y + y) % NY * NZ + self.z) * NX + (self.x + x) % NX, self.rep
+
     def along_y(self, by):
         return (self.blk + by * NX * NZ) % (NX * NZ * NY), self.rep
 
@@ -138,14 +145,16 @@
 
     def greet(self):
         there = [self.along_z(o) for o in range(1, NZ)]
-        there += [self.along_x(o) for o in range(1, NX)]
-        there += [self.along_y(o) for o in range(1, NY)]
+        there += [self.along_xy(o) for o in range(1, NX * NY)]
         there += [self.along_blk(o) for o in (1, 2, -1, -2)]
         there += [self.partner()]
         barrier = pltpu.get_barrier_semaphore()
         for device in there:
             pl.semaphore_signal(barrier, inc=1, device_id=device, device_id_type=MESH)
-        pl.semaphore_wait(barrier, len(there))
+        return len(there)
+
+    def meet(self, count):
+        pl.semaphore_wait(pltpu.get_barrier_semaphore(), count)
 
 
 def send(src, dst, sems, index, device):
@@ -161,12 +170,12 @@
     return copy
 
 
-def pick_weights(place, marks):
+def pick_weights(first, marks):
     ids = lax.broadcasted_iota(jnp.int32, (G, T), 0) * T + lax.broadcasted_iota(jnp.int32, (G, T), 1)
     named = jnp.where(marks > 0.5, 1.0, 0.0)
     weights = []
     for c in range(OWN):
-        own = place.blk * OWN + c
+        own = first + c
         here = jnp.sum(jnp.where(ids == own, named, 0.0), keepdims=True)
         rank = jnp.sum(jnp.where(ids < own, named, 0.0), keepdims=True)
         weights.append([here * jnp.where(jnp.abs(rank - s) < 0.5, 1.0, 0.0) for s in range(HOT)])
@@ -206,11 +215,11 @@
         self.joint, self.width = x.shape
         self.lead = self.joint - T
 
-    def place_rows(self, k, mine, other):
+    def place_rows(self, k, mine, other, line=None):
         rs = slice(k * T, (k + 1) * T)
         self.x[rs, :T] = mine[:T].astype(jnp.bfloat16)
         self.x[rs, T:] = other[:T].astype(jnp.bfloat16)
-        obs = jnp.broadcast_to(mine[T : T + 1], (T, T))
+        obs = jnp.broadcast_to(mine[T : T + 1] if line is None else line, (T, T))
         self.work[rs, self.joint :] = jnp.transpose(obs)
         wide = self.x[rs, :].astype(jnp.float32)
         self.squares[rs, :] = jnp.broadcast_to(jnp.sum(wide * wide, axis=1, keepdims=True), (T, T))
@@ -239,10 +248,10 @@
             self.covariance(rows, cols)
         self.piv[...] = self.work[:T, :T]
 
-    def near_pivot(self, k):
+    def near_pivot(self, k, half=False):
         w = self.work
         a, b = k * T, (k + 1) * T
-        negative_inverse(self.piv)
+        negative_inverse(self.piv, half)
         minv = -self.piv[...]
         self.inverse[k] = minv
         groups = [(self.lead, self.joint + T)]
@@ -296,17 +305,23 @@
             e = -right[rs, :T] if k < 4 else jnp.where(diagonal(), 1.0, 0.0)
             alpha = right[rs, T:] if k < 4 else jnp.zeros((T, T), jnp.float32)
             v = dot32(e, u)
-            self.ext[rs, :T] = e
-            self.ext[rs, T:] = jnp.where(lane == 0, v, jnp.where(lane == 1, alpha, 0.0))
-            w[rs, :T] = -dot32(e, inner)
-            w[rs, T : 2 * T] = jnp.where(lane == 0, alpha, jnp.where(lane == 1, v, 0.0))
+            left = (-dot32(e, inner), jnp.where(lane == 0, alpha, jnp.where(lane == 1, v, 0.0)))
+            for i, term in enumerate(left + (e, jnp.where(lane == 0, v, jnp.where(lane == 1, alpha, 0.0)))):
+                cols = slice(i % 2 * T, (i % 2 + 1) * T)
+                self.ext[i // 2 * 2, rs, cols], self.ext[i // 2 * 2 + 1, rs, cols] = split(term)
         return -0.5 * (quad + logs) - 0.5 * T * math.log(2.0 * math.pi)
 
     def grad_rows(self, k):
         rs = slice(k * T, (k + 1) * T)
         col = lax.broadcasted_iota(jnp.int32, (T, self.joint), 1)
         row = lax.broadcasted_iota(jnp.int32, (T, self.joint), 0)
-        m = dot32(self.work[rs, : 2 * T], self.ext[...], ((1,), (1,)))
+        across = (((1,), (1,)), ((), ()))
+        m = add_up(
+            [
+                lax.dot_general(self.ext[i, rs, :], self.ext[j], across, preferred_element_type=jnp.float32)
+                for i, j in ((0, 3), (1, 2), (0, 2))
+            ]
+        )
         sym = jnp.where(col == row + k * T, 0.0, m * self.kern[rs, :] * (-0.5 / self.width)).astype(jnp.bfloat16)
         rowsum = jnp.sum(sym.astype(jnp.float32), axis=1, keepdims=True)
         part = jnp.dot(sym, self.x[...], preferred_element_type=jnp.float32)
@@ -317,85 +332,116 @@
     return lax.broadcasted_iota(jnp.int32, (T, T), 0) == lax.broadcasted_iota(jnp.int32, (T, T), 1)
 
 
-def whole_kernel(cond_ref, own_ref, value_ref, out_ref,
-                 m0, m1, m2, mz, mx, my,
-                 near_mine, near_other, hot_mine, hot_other, slots, zgot, xgot, ygot, held,
+def whole_kernel(cond_ref, feat_ref, obs_ref, value_ref, out_ref,
+                 m0, m1, mz, mxy, own, row, obs0, obs1, obs2, oz, oy, ox,
+                 near_mine, near_other, hot_mine, hot_other, slots, zgot, ygot, held, whole,
                  x, kern, work, piv, inverse, right, ext, squares,
                  back_mine, back_other, back_got, side_mine, side_other, side_got, near_out, near_got,
                  slots2, hot2, zgot2, xgot2, ygot2, held2,
-                 msem, nsem, psem, zsem, xsem, ysem, gsem, fsem,
+                 msem, rsem, osem, nsem, psem, zsem, ysem, xsem, gsem, fsem,
                  nsem2, psem2, zsem2, xsem2, ysem2, gsem2):
     place = Place()
     terms = Terms(x, kern, work, piv, inverse, right, ext, squares)
-    place.greet()
+    greeted = place.greet()
     ids = lax.broadcasted_iota(jnp.int32, (G, T), 0) * T + lax.broadcasted_iota(jnp.int32, (G, T), 1)
     marks = jnp.zeros((G, T), jnp.float32)
     for c in range(OWN):
         for k in (2, 3):
             marks = jnp.where(ids == cond_ref[c, k], 1.0, marks)
     m0[...] = marks
+    obs_rows = obs_ref[...].astype(jnp.float32)
+    for c in range(OWN):
+        own[c, :T, :] = feat_ref[c * T : (c + 1) * T, :]
+        own[c, T:, :] = jnp.broadcast_to(obs_rows[c : c + 1, :], (PACK - T, T)).astype(jnp.bfloat16)
+    near_mine[:OWN] = own[...]
+    for c in range(OWN):
+        row[NX - 1, c * T : (c + 1) * T, :] = feat_ref[c * T : (c + 1) * T, :]
+    place.meet(greeted)
     stage = start_stage(m0, mz, msem.at[:, pl.ds(0, NZ - 1)], place.along_z, NZ)
+    rows = start_stage(feat_ref, row, rsem, place.along_x, NX)
     near = []
     for by in (1, 2):
-        near.append(send(own_ref, near_mine.at[pl.ds(by * OWN, OWN)], nsem, by - 1, place.along_blk(by)))
-    early = [send(own_ref, near_other.at[pl.ds(0, OWN)], psem, 0, place.partner())]
-    near_mine[:OWN] = own_ref[...]
+        near.append(send(own, near_mine.at[pl.ds(by * OWN, OWN)], nsem, by - 1, place.along_blk(by)))
+    early = [send(own, near_other.at[pl.ds(0, OWN)], psem, 0, place.partner())]
     m1[...] = end_stage(stage, m0[...], mz)
-    stage = start_stage(m1, mx, msem.at[:, pl.ds(NZ - 1, NX - 1)], place.along_x, NX)
+    stage = start_stage(m1, mxy, msem.at[:, pl.ds(NZ - 1, NX * NY - 1)], place.along_xy, NX * NY)
     for by in (1, 2):
         near[by - 1].wait()
         part = pl.ds(by * OWN, OWN)
         early.append(send(near_mine.at[part], near_other.at[part], psem, by, place.partner()))
-    m2[...] = end_stage(stage, m1[...], mx)
-    stage = start_stage(m2, my, msem.at[:, pl.ds(NZ + NX - 2, NY - 1)], place.along_y, NY)
-    marks = end_stage(stage, m2[...], my)
-    picks = pick_weights(place, marks)
-    for s in range(HOT):
-        slots[s] = weighted([p[s] for p in picks], [own_ref[c] for c in range(OWN)]).astype(jnp.bfloat16)
-    stage = start_scatter(place, slots, zgot, zsem)
-    for copy in early:
-        copy.wait()
     near_ids = []
     for s in range(OWN * (NEAR + 1)):
         near_ids.append((place.blk + NX * NZ * NY - s // OWN) % (NX * NZ * NY) * OWN + s % OWN)
     near_w = [[jnp.where(cond_ref[place.rep, k] == i, 1.0, 0.0) for i in near_ids] for k in range(2)]
     own_w = [jnp.where(place.rep == c, 1.0, 0.0) for c in range(OWN)]
     count = len(near_ids)
+    early[0].wait()
+    terms.place_rows(
+        4,
+        weighted(own_w, [near_mine[c] for c in range(OWN)]),
+        weighted(own_w, [near_other[c] for c in range(OWN)]),
+    )
+    for copy in early[1:]:
+        copy.wait()
     for k in range(2):
         terms.place_rows(
             k,
             weighted(near_w[k], [near_mine[s] for s in range(count)]),
             weighted(near_w[k], [near_other[s] for s in range(count)]),
         )
-    terms.place_rows(
-        4,
-        weighted(own_w, [near_mine[c] for c in range(OWN)]),
-        weighted(own_w, [near_other[c] for c in range(OWN)]),
-    )
     terms.near_first()
-    terms.near_pivot(0)
-    held[0] = end_stage(stage, slots[place.z], zgot).astype(held.dtype)
-    stage = start_stage(held.at[0], xgot, xsem, place.along_x, NX)
-    held[1] = end_stage(stage, held[0], xgot).astype(held.dtype)
-    stage = start_stage(held.at[1], ygot, ysem, place.along_y, NY)
-    held[2] = end_stage(stage, held[1], ygot).astype(held.dtype)
-    stage = start_gather(place, held.at[2], hot_mine, gsem)
-    passed = [send(held.at[2], hot_other.at[place.z], fsem, 0, place.partner())]
-    terms.near_pivot(1)
-    for o in range(1, NZ):
-        stage[o - 1].wait()
-        slot = (place.z + NZ - o) % NZ
-        passed.append(send(hot_mine.at[slot], hot_other.at[slot], fsem, o, place.partner()))
+    marks = end_stage(stage, m1[...], mxy)
+    for copy in rows:
+        copy.wait()
+    quarter = pl.ds(place.x * (T // NX), T // NX)
+    picks = pick_weights(place.blk * OWN, marks)
+    row_picks = [picks]
+    blocks = [row[NX - 1, pl.ds(c * T + place.x * (T // NX), T // NX), :] for c in range(OWN)]
+    for o in range(1, NX):
+        row_picks.append(pick_weights(place.along_x(NX - o)[0] * OWN, marks))
+        blocks += [row[o - 1, pl.ds(c * T + place.x * (T // NX), T // NX), :] for c in range(OWN)]
+    for s in range(HOT):
+        slots[s] = weighted([p[s] for ps in row_picks for p in ps], blocks).astype(jnp.bfloat16)
+    obs = jnp.zeros((HOT, T), jnp.float32)
+    for s in range(HOT):
+        line = weighted([p[s] for p in picks], [obs_rows[c : c + 1, :] for c in range(OWN)])
+        obs = jnp.where(lax.broadcasted_iota(jnp.int32, (HOT, T), 0) == s, line, obs)
+    obs0[...] = obs
+    stage = start_scatter(place, slots, zgot, zsem)
+    obs_stage = start_stage(obs0, oz, osem.at[:, pl.ds(0, NZ - 1)], place.along_z, NZ)
     named = jnp.where(marks > 0.5, 1.0, 0.0)
     hot_w = []
     for k in (2, 3):
         rank = jnp.sum(jnp.where(ids < cond_ref[place.rep, k], named, 0.0), keepdims=True)
         hot_w.append([jnp.where(jnp.abs(rank - s) < 0.5, 1.0, 0.0) for s in range(HOT)])
+    negative_inverse(piv, half=True)
+    held[0] = end_stage(stage, slots[place.z], zgot).astype(held.dtype)
+    obs1[...] = end_stage(obs_stage, obs0[...], oz)
+    stage = start_stage(held.at[0], ygot, ysem, place.along_y, NY)
+    obs_stage = start_stage(obs1, oy, osem.at[:, pl.ds(NZ - 1, NY - 1)], place.along_y, NY)
+    terms.near_pivot(0, half=True)
+    held[1] = end_stage(stage, held[0], ygot).astype(held.dtype)
+    obs2[...] = end_stage(obs_stage, obs1[...], oy)
+    whole[quarter, :] = held[1]
+    stage = [send(held.at[1], whole.at[quarter], xsem, o - 1, place.along_x(o)) for o in range(1, NX)]
+    obs_stage = start_stage(obs2, ox, osem.at[:, pl.ds(NZ + NY - 2, NX - 1)], place.along_x, NX)
+    negative_inverse(piv, half=True)
+    for copy in stage:
+        copy.wait()
+    hot_obs = end_stage(obs_stage, obs2[...], ox)
+    stage = start_gather(place, whole, hot_mine, gsem)
+    passed = [send(whole, hot_other.at[place.z], fsem, 0, place.partner())]
+    terms.near_pivot(1, half=True)
+    for o in range(1, NZ):
+        stage[o - 1].wait()
+        slot = (place.z + NZ - o) % NZ
+        passed.append(send(hot_mine.at[slot], hot_other.at[slot], fsem, o, place.partner()))
     mine = [weighted(w, [hot_mine[s] for s in range(HOT)]) for w in hot_w]
+    lines = [weighted(w, [hot_obs[s : s + 1, :] for s in range(HOT)]) for w in hot_w]
     for copy in passed:
         copy.wait()
     for k in (0, 1):
-        terms.place_rows(2 + k, mine[k], weighted(hot_w[k], [hot_other[s] for s in range(HOT)]))
+        terms.place_rows(2 + k, mine[k], weighted(hot_w[k], [hot_other[s] for s in range(HOT)]), lines[k])
     value_ref[...] = terms.finish()
     grads = [terms.grad_rows(k) for k in (2, 3)]
     for s in range(HOT):
@@ -403,16 +449,17 @@
         back_mine[s] = total[:, :T]
         back_other[s] = total[:, T:]
     hot_copy = send(back_other, back_got, psem2, 0, place.partner())
-    grads = [terms.grad_rows(k) for k in (0, 1, 4)]
+    grads = [terms.grad_rows(0)]
+    hot_copy.wait()
+    slots2[...] = (back_mine[...].astype(jnp.float32) + back_got[...].astype(jnp.float32)).astype(jnp.bfloat16)
+    stage = start_scatter(place, slots2, zgot2, zsem2)
+    grads += [terms.grad_rows(k) for k in (1, 4)]
     for s in range(count):
         weights = [near_w[0][s], near_w[1][s]] + ([own_w[s]] if s < OWN else [])
         total = weighted(weights, grads).astype(jnp.bfloat16)
         side_mine[s] = total[:, :T]
         side_other[s] = total[:, T:]
     side_copy = send(side_other, side_got, psem2, 1, place.partner())
-    hot_copy.wait()
-    slots2[...] = (back_mine[...].astype(jnp.float32) + back_got[...].astype(jnp.float32)).astype(jnp.bfloat16)
-    stage = start_scatter(place, slots2, zgot2, zsem2)
     side_copy.wait()
     part = pl.ds(OWN, OWN * NEAR)
     near_out[...] = (side_mine[part].astype(jnp.float32) + side_got[part].astype(jnp.float32)).astype(jnp.bfloat16)
@@ -457,8 +504,6 @@
     width = features.shape[1]
     joint = (cond_ids.shape[1] + 1) * T
     count = OWN * (NEAR + 1)
-    obs = jnp.broadcast_to(observations[:, None, :], (per_dev, PACK - T, T))
-    own = jnp.concatenate([features.reshape(per_dev, T, width), obs], axis=1)
     ring = [NZ - 1, NX - 1, NY - 1]
     value, grad = pl.pallas_call(
         whole_kernel,
@@ -466,13 +511,17 @@
             jax.ShapeDtypeStruct((G, T), jnp.float32),
             jax.ShapeDtypeStruct((per_dev * T, width), jnp.float32),
         ),
-        in_specs=[pl.BlockSpec(memory_space=pltpu.SMEM), VMEM],
+        in_specs=[pl.BlockSpec(memory_space=pltpu.SMEM), VMEM, VMEM],
         out_specs=(VMEM, VMEM),
-        scratch_shapes=[full(G, T)] * 3
-        + [full(n, G, T) for n in ring]
+        scratch_shapes=[full(G, T)] * 2
+        + [full(n, G, T) for n in (NZ - 1, NX * NY - 1)]
+        + [half(OWN, PACK, T), half(NX, OWN * T, T)]
+        + [full(HOT, T)] * 3
+        + [full(n - 1, HOT, T) for n in (NZ, NY, NX)]
         + [half(count, PACK, T)] * 2
-        + [half(HOT, PACK, T)] * 3
-        + [half(n, PACK, T) for n in ring + [3]]
+        + [half(HOT, T, T)] * 2
+        + [half(n, T // NX, T) for n in (HOT, NZ - 1, NY - 1, 2)]
+        + [half(T, T)]
         + [
             half(joint, 2 * T),
             full(joint, joint),
@@ -480,7 +529,7 @@
             full(T, T),
             full(2, T, T),
             full(joint - T, 2 * T),
-            full(joint, 2 * T),
+            half(4, joint, 2 * T),
             full(joint, T),
         ]
         + [half(HOT, T, T)] * 3
@@ -488,13 +537,14 @@
         + [half(OWN * NEAR, T, T)] * 2
         + [half(HOT, T, T)] * 2
         + [half(n, T, T) for n in ring + [3]]
-        + [dma(n) for n in (sum(ring), NEAR, NEAR + 1, *ring, NZ - 1, NZ)]
+        + [dma(n) for n in (NZ + NX * NY - 2, NX - 1, sum(ring), NEAR, NEAR + 1)]
+        + [dma(n) for n in (NZ - 1, NY - 1, NX - 1, NZ - 1, NZ)]
         + [dma(n) for n in (NEAR, 2, *ring, NZ - 1)],
         compiler_params=pltpu.CompilerParams(
             collective_id=0, has_side_effects=True, vmem_limit_bytes=50 << 20
         ),
         name="block_vecchia",
-    )(cond_ids, own)
+    )(cond_ids, features, observations)
     return (value[0, :1], grad)
 
 

time: 98.2 us -> 96.1 us (0.979)
  Pallas kernels: 94 us -> 91.5 us
  local copies, waits for them, and re-layouts: 1.82 us -> 3.33 us
    pallas_call x1, Pallas kernels: 94 us -> 91.5 us  [body(): pl.pallas_call(whole_kernel, out_shape=(jax.ShapeDtypeStruct((G, T), jnp....]
    unnamed x5 -> x7, local copies, waits for them, and re-layouts: 1.31 us -> 2.82 us
where the time goes in v3:
time: 96.1 us; the launch traced here: 95.5 us
  Pallas kernels  91.5 us (95%)
  local copies, waits for them, and re-layouts  3.33 us (3%)
    pallas_call x1, Pallas kernels, body(): pl.pallas_call(whole_kernel, out_shape=(jax.ShapeDtypeStruct((G, T), jnp....  91.5 us
    unnamed x7, local copies, waits for them, and re-layouts  2.82 us

profile of v3, /device:TPU:4, one launch (start us, length us, event | category | flops | bytes accessed | tf_op | source)
XLA Modules:
  0.0 95.5 jit_solution(12047048645277014575)
XLA Ops:
  0.6 0.0 copy-start
  0.6 0.8 copy-done
  1.5 0.0 copy-start.1
  1.5 0.7 copy-done.1
  2.1 0.0 copy-start.2
  2.2 0.7 copy-done.2
  2.8 91.5 %block_vecchia.1 = (f32[8,128]{1,0:T(8,128)S(1)}, f32[256,128]{1,0:T(8,128)S(1)}) custom-call(s32[2,4]{1,0:T(2,128)S(1)} %copy-done.1, bf16[256,128]{1,0:T(8,128)(2,1)S(1)} %copy-done, bf16[2,128]{1,0:T(2,128)(2,1)S(1)} %copy-done.2), custom_call_target="tpu_custom_call" | custom-call | tf_op jit(solution)/shard_map/block_vecchia/pallas_call | solution.py:508
  94.3 0.5 slice.3
  94.8 0.7 copy.6
Async XLA Ops:
  0.6 0.8 copy-start
  1.5 0.7 copy-start.1
  2.1 0.7 copy-start.2

commit v4 on v3

--- a/solution.py
+++ b/solution.py
@@ -248,10 +248,9 @@
             self.covariance(rows, cols)
         self.piv[...] = self.work[:T, :T]
 
-    def near_pivot(self, k, half=False):
+    def near_update(self, k):
         w = self.work
         a, b = k * T, (k + 1) * T
-        negative_inverse(self.piv, half)
         minv = -self.piv[...]
         self.inverse[k] = minv
         groups = [(self.lead, self.joint + T)]
@@ -419,19 +418,20 @@
     obs1[...] = end_stage(obs_stage, obs0[...], oz)
     stage = start_stage(held.at[0], ygot, ysem, place.along_y, NY)
     obs_stage = start_stage(obs1, oy, osem.at[:, pl.ds(NZ - 1, NY - 1)], place.along_y, NY)
-    terms.near_pivot(0, half=True)
+    negative_inverse(piv, half=True)
     held[1] = end_stage(stage, held[0], ygot).astype(held.dtype)
     obs2[...] = end_stage(obs_stage, obs1[...], oy)
     whole[quarter, :] = held[1]
     stage = [send(held.at[1], whole.at[quarter], xsem, o - 1, place.along_x(o)) for o in range(1, NX)]
     obs_stage = start_stage(obs2, ox, osem.at[:, pl.ds(NZ + NY - 2, NX - 1)], place.along_x, NX)
-    negative_inverse(piv, half=True)
+    terms.near_update(0)
     for copy in stage:
         copy.wait()
     hot_obs = end_stage(obs_stage, obs2[...], ox)
     stage = start_gather(place, whole, hot_mine, gsem)
     passed = [send(whole, hot_other.at[place.z], fsem, 0, place.partner())]
-    terms.near_pivot(1, half=True)
+    negative_inverse(piv)
+    terms.near_update(1)
     for o in range(1, NZ):
         stage[o - 1].wait()
         slot = (place.z + NZ - o) % NZ

time: 96.1 us -> 95.6 us (level)
  no operation moved by 1% of the time
where the time goes in v4:
time: 95.6 us; the launch traced here: 95.4 us
  Pallas kernels  91.4 us (96%)
  local copies, waits for them, and re-layouts  3.33 us (3%)
    pallas_call x1, Pallas kernels, body(): pl.pallas_call(whole_kernel, out_shape=(jax.ShapeDtypeStruct((G, T), jnp....  91.4 us
    unnamed x7, local copies, waits for them, and re-layouts  2.82 us

profile of v4, /device:TPU:4, one launch (start us, length us, event | category | flops | bytes accessed | tf_op | source)
XLA Modules:
  0.0 95.4 jit_solution(4995853287715436276)
XLA Ops:
  0.6 0.0 copy-start
  0.6 0.8 copy-done
  1.5 0.0 copy-start.1
  1.5 0.7 copy-done.1
  2.1 0.0 copy-start.2
  2.2 0.7 copy-done.2
  2.8 91.4 %block_vecchia.1 = (f32[8,128]{1,0:T(8,128)S(1)}, f32[256,128]{1,0:T(8,128)S(1)}) custom-call(s32[2,4]{1,0:T(2,128)S(1)} %copy-done.1, bf16[256,128]{1,0:T(8,128)(2,1)S(1)} %copy-done, bf16[2,128]{1,0:T(2,128)(2,1)S(1)} %copy-done.2), custom_call_target="tpu_custom_call" | custom-call | tf_op jit(solution)/shard_map/block_vecchia/pallas_call | solution.py:508
  94.2 0.5 slice.3
  94.8 0.7 copy.6
Async XLA Ops:
  0.6 0.8 copy-start
  1.5 0.7 copy-start.1
  2.1 0.7 copy-start.2
